TPU v7x, 128 devices: a whole 4x4x4 slice. The times are simulated.
128 devices in a mesh: row: 16 (over z, x_hi, core), col: 8 (over y, x_lo).
Axes of the slice: x: 4 (x_hi: 2, x_lo: 2; x = x_hi * 2 + x_lo), y: 4, z: 4, core: 2. Of those that a mesh axis runs over, the one named last changes fastest.
Arguments:
- queries: bfloat16 [1024, 8192], P('col', 'row'), may hold values from -8 to 8
- cache_keys: bfloat16 [8, 131072, 128], P(None, ('row', 'col')), may hold values from -8 to 8
- cache_values: bfloat16 [8, 131072, 128], P(None, ('row', 'col')), may hold values from -6 to 6
- stretch_keys: bfloat16 [8, 1024, 128], P(None, 'col'), may hold values from -8 to 8
- stretch_values: bfloat16 [8, 1024, 128], P(None, 'col'), may hold values from -6 to 6
- block_lists: int32 [8, 8, 64], replicated, may hold values from 0 to 1023, as said below
- out_weight: bfloat16 [8192, 8192], P('row', 'col'), may hold values from -0.5 to 0.5
- residual: bfloat16 [1024, 8192], P('row', 'col'), may hold values from -6 to 6
- norm_gain: bfloat16 [8192], P('col'), may hold values from 0.25 to 1.75
- gate_weight: bfloat16 [8192, 28672], P('col', 'row'), may hold values from -0.0625 to 0.0625
- up_weight: bfloat16 [8192, 28672], P('col', 'row'), may hold values from -0.0625 to 0.0625
- down_weight: bfloat16 [28672, 8192], P('row', 'col'), may hold values from -0.03125 to 0.03125
Outputs:
- layer_out: bfloat16 [1024, 8192], P('row', 'col')
Inputs may be any that keep to these rules, and one draw needn't show every extreme that they name: `block_lists`: each list names 64 different cache blocks; device k of row+col holds cache blocks k * (8) to (k + 1) * 8 - 1, and no two blocks of one list lie on the same device. Every list holds block 0 and block 1023.
All inputs are finite; a program needn't handle non-finite values.
Results may differ from a plain program's by a relative error of at most 0.0085.
Values may be sent and summed in bfloat16 or wider, within the bound.
No kernel may reach another device: no remote copies, remote signals or barrier semaphores. Data moves between devices by JAX's collectives and lax.ppermute only.
A program may use at most 128 MiB of HBM per device.

v0:
```python
import math
import jax
import jax.numpy as jnp
from jax import lax
from jax.sharding import PartitionSpec as P

D = 8192
KV_HEADS = 8
HEAD_DIM = 128
BLK = 128
GROUP = 8


def local(
    queries,
    cache_keys,
    cache_values,
    stretch_keys,
    stretch_values,
    block_lists,
    out_weight,
    residual,
    norm_gain,
    gate_weight,
    up_weight,
    down_weight,
):
    row_count = lax.axis_size("row")
    col_count = lax.axis_size("col")
    row_index = lax.axis_index("row")
    col_index = lax.axis_index("col")
    device_count = row_count * col_count
    my_index = row_index * col_count + col_index
    local_blocks = cache_keys.shape[1] // BLK
    heads_here = queries.shape[1] // HEAD_DIM
    list_length = block_lists.shape[2]
    my_group = row_index * heads_here // GROUP
    scaling = 1.0 / math.sqrt(HEAD_DIM)
    targets = jnp.arange(device_count, dtype=jnp.int32)
    target_group = targets // col_count * heads_here // GROUP
    target_lists = block_lists[targets % col_count, target_group]
    holders = target_lists // local_blocks
    matched = holders == my_index
    found_any = jnp.any(matched, axis=1)
    within = jnp.sum(jnp.where(matched, target_lists % local_blocks, 0), axis=1)
    source_rows = target_group * local_blocks + within
    flat_keys = cache_keys.reshape(KV_HEADS * local_blocks, BLK, HEAD_DIM)
    flat_values = cache_values.reshape(KV_HEADS * local_blocks, BLK, HEAD_DIM)
    outgoing = jnp.concatenate([flat_keys[source_rows], flat_values[source_rows]], axis=2)
    outgoing = jnp.where(found_any[:, None, None], outgoing, jnp.zeros_like(outgoing))
    arrived = lax.all_to_all(outgoing, ("row", "col"), split_axis=0, concat_axis=0, tiled=True)
    my_list = block_lists[col_index, my_group]
    fetched = arrived[my_list // local_blocks].reshape(list_length * BLK, 2 * HEAD_DIM)
    far_keys = fetched[:, :HEAD_DIM]
    far_values = fetched[:, HEAD_DIM:]
    query_rows = queries.reshape(BLK * heads_here, HEAD_DIM)
    far_scores = jnp.dot(query_rows, far_keys.T, preferred_element_type=jnp.float32) * scaling
    run_max = jnp.max(far_scores, axis=1)
    far_exp = jnp.exp(far_scores - run_max[:, None])
    run_sum = jnp.sum(far_exp, axis=1)
    run_acc = jnp.dot(far_exp.astype(jnp.bfloat16), far_values, preferred_element_type=jnp.float32)
    query_pos = col_index * BLK + jnp.arange(BLK * heads_here, dtype=jnp.int32) // heads_here
    own_keys = lax.dynamic_index_in_dim(stretch_keys, my_group, 0, keepdims=False)
    own_values = lax.dynamic_index_in_dim(stretch_values, my_group, 0, keepdims=False)
    piece_keys = lax.all_gather(own_keys, "col", axis=0, tiled=True)
    piece_values = lax.all_gather(own_values, "col", axis=0, tiled=True)
    scores = jnp.dot(query_rows, piece_keys.T, preferred_element_type=jnp.float32) * scaling
    key_pos = jnp.arange(piece_keys.shape[0], dtype=jnp.int32)
    allowed = key_pos[None, :] <= query_pos[:, None]
    scores = jnp.where(allowed, scores, -1e30)
    new_max = jnp.maximum(run_max, jnp.max(scores, axis=1))
    decays = jnp.exp(run_max - new_max)
    weights = jnp.where(allowed, jnp.exp(scores - new_max[:, None]), 0.0)
    new_sum = run_sum * decays + jnp.sum(weights, axis=1)
    new_acc = run_acc * decays[:, None] + jnp.dot(
        weights.astype(jnp.bfloat16), piece_values, preferred_element_type=jnp.float32
    )
    attended = (new_acc / new_sum[:, None]).astype(jnp.bfloat16).reshape(BLK, heads_here * HEAD_DIM)
    all_attended = lax.all_gather(attended, "col", axis=0, tiled=True)
    projected = lax.psum_scatter(
        jnp.dot(all_attended, out_weight, preferred_element_type=jnp.float32),
        "row",
        scatter_dimension=0,
        tiled=True,
    )
    stream = residual.astype(jnp.float32) + projected
    squares = lax.psum(jnp.sum(stream * stream, axis=1), "col")
    normed = (
        stream * lax.rsqrt(squares / D + 1e-05)[:, None] * norm_gain.astype(jnp.float32)
    ).astype(jnp.bfloat16)
    block_piece = lax.all_gather(normed, "row", axis=0, tiled=True)
    gate_part = jnp.dot(block_piece, gate_weight, preferred_element_type=jnp.float32)
    up_part = jnp.dot(block_piece, up_weight, preferred_element_type=jnp.float32)
    partials = jnp.concatenate([gate_part, up_part], axis=1)
    hidden_width = gate_weight.shape[1]
    summed = lax.psum(partials, "col")
    hidden = (jax.nn.silu(summed[:, :hidden_width]) * summed[:, hidden_width:]).astype(jnp.bfloat16)
    down_terms = jnp.dot(hidden, down_weight, preferred_element_type=jnp.float32)
    mlp_part = lax.psum_scatter(down_terms, "row", scatter_dimension=0, tiled=True)
    return (stream + mlp_part).astype(jnp.bfloat16)


def solution(mesh):
    in_specs = (
        P("col", "row"),
        P(None, ("row", "col"), None),
        P(None, ("row", "col"), None),
        P(None, "col", None),
        P(None, "col", None),
        P(),
        P("row", "col"),
        P("row", "col"),
        P("col"),
        P("col", "row"),
        P("col", "row"),
        P("row", "col"),
    )
    out_specs = P("row", "col")
    return jax.shard_map(local, mesh=mesh, in_specs=in_specs, out_specs=out_specs, check_vma=False)
```

profile of v0, /device:TPU:0, one launch (start us, length us, event | category | flops | bytes accessed | tf_op | source)
XLA Modules:
  0.0 1105.7 jit_solution(4571468520694999564)
XLA Ops:
  6.6 1.9 gather_fusion
  8.7 3.1 gather_fusion.2
  11.8 4.6 gather_fusion.1
  16.4 8.2 maximum_select_fusion
  24.6 11.7 %all-to-all-start = ((bf16[128,128,256]{2,1,0:T(8,128)(2,1)}), bf16[128,128,256]{2,1,0:T(8,128)(2,1)}, u32[]{:S(2)}, u32[]{:S(2)}) async-start(bf16[128,128,256]{2,1,0:T(8,128)(2,1)} %maximum_select_fusion), calls=%async_computation | async-start | bytes 16777216 | tf_op jit(solution)/shard_map/all_to_all | solution.py:51
  36.5 0.7 fusion.41
  37.2 0.8 constant_dynamic-slice_fusion.1
  38.0 0.8 constant_dynamic-slice_fusion
  38.7 118.4 %all-gather.1 = bf16[1,1024,128]{2,1,0:T(8,128)(2,1)S(1)} all-gather(bf16[1,128,128]{2,1,0:T(8,128)(2,1)S(1)} %constant_dynamic-slice_fusion), channel_id=3, replica_groups=mesh['row'=16,'col'=8] {'col'}, dimensions={1}, use_global_device_ids=true | all-gather | bytes 294912 | tf_op jit(solution)/shard_map/all_gather | solution.py:66
  157.1 28.9 %all-gather = bf16[1,1024,128]{2,1,0:T(8,128)(2,1)S(1)} all-gather(bf16[1,128,128]{2,1,0:T(8,128)(2,1)S(1)} %constant_dynamic-slice_fusion.1), channel_id=2, replica_groups=mesh['row'=16,'col'=8] {'col'}, dimensions={1}, use_global_device_ids=true | all-gather | bytes 294912 | tf_op jit(solution)/shard_map/all_gather | solution.py:65
  186.5 6.1 gather_fusion.3
  192.6 9.6 multiply_reduce_fusion
  202.2 8.8 fusion
  211.0 0.6 fusion.11
  211.6 7.7 fusion.15
  219.3 0.8 fusion.14
  220.1 0.7 reshape.273
  220.9 39.3 %all-gather.5.cloned.1.call-done = bf16[1024,512]{1,0:T(8,128)(2,1)} async-done(((bf16[128,512]{1,0:T(8,128)(2,1)}), bf16[1024,512]{1,0:T(8,128)(2,1)}) %all-gather.5.cloned.1.call-update) | async-done | bytes 1048592 | tf_op jit(solution)/shard_map/all_gather | solution.py:79
  260.3 4.7 fusion.50
  265.1 0.6 copy-done.6
  265.7 79.7 %reduce-scatter.3.cloned.1.call-done = f32[64,1024]{1,0:T(8,128)} async-done(((f32[1024,1024]{1,0:T(8,128)}), f32[64,1024]{1,0:T(8,128)}) %reduce-scatter.3.cloned.1.call-update) | async-done | bytes 262160 | tf_op jit(solution)/shard_map/reduce_scatter | solution.py:80
  345.4 1.1 multiply_reduce_fusion.1
  346.4 18.8 %psum.14 = f32[64]{0:T(128)S(1)} all-reduce(f32[64]{0:T(128)S(1)} %multiply_reduce_fusion.1), channel_id=1, replica_groups=mesh['row'=16,'col'=8] {'col'}, use_global_device_ids=true, to_apply=%region_8.9 | all-reduce | flops 64 | bytes 512 | tf_op jit(solution)/shard_map/psum | solution.py:87
  365.2 1.7 multiply_convert_fusion
  367.2 44.7 %all-gather.7.cloned.1.call-done = bf16[1024,1024]{1,0:T(8,128)(2,1)} async-done(((bf16[64,1024]{1,0:T(8,128)(2,1)}), bf16[1024,1024]{1,0:T(8,128)(2,1)}) %all-gather.7.cloned.1.call-update) | async-done | bytes 2097168 | tf_op jit(solution)/shard_map/all_gather | solution.py:91
  412.0 6.8 fusion.52
  418.8 4.0 fusion.51
  422.7 5.7 pad_maximum_fusion
  428.5 574.8 %all-reduce.2.cloned.1.call-done = f32[1024,3584]{1,0:T(8,128)} async-done(((f32[1024,3584]{1,0:T(8,128)}), f32[1024,3584]{1,0:T(8,128)}) %all-reduce.2.cloned.1.call-update) | async-done | bytes 14680080 | tf_op jit(solution)/shard_map/psum | solution.py:96
  1003.3 12.3 %fusion.5 = f32[1024,1024]{1,0:T(8,128)} fusion(bf16[1792,1024]{1,0:T(8,128)(2,1)} %param.23, f32[1024,3584]{1,0:T(8,128)} %all-reduce.2.cloned.1.call-done), kind=kOutput, calls=%fused_computation.13 | convolution fusion | flops 3769106432 | bytes 22544384 | tf_op jit(solution)/shard_map/dot_general | solution.py:98
  1015.7 81.9 %reduce-scatter.5.cloned.1.call-done = f32[64,1024]{1,0:T(8,128)} async-done(((f32[1024,1024]{1,0:T(8,128)}), f32[64,1024]{1,0:T(8,128)}) %reduce-scatter.5.cloned.1.call-update) | async-done | bytes 262160 | tf_op jit(solution)/shard_map/reduce_scatter | solution.py:99
  1097.5 1.6 add_convert_fusion
  (41 shorter events, 1.4 us)
Async XLA Ops:
  6.5 2.2 copy-start
  24.6 11.8 %copy-start.5 = (bf16[128,512]{1,0:T(8,128)(2,1)S(1)}, bf16[128,512]{1,0:T(8,128)(2,1)}, u32[]{:S(2)}) copy-start(bf16[128,512]{1,0:T(8,128)(2,1)} %param.12) | copy-start | bytes 393220
  24.6 161.9 %all-to-all-start = ((bf16[128,128,256]{2,1,0:T(8,128)(2,1)}), bf16[128,128,256]{2,1,0:T(8,128)(2,1)}, u32[]{:S(2)}, u32[]{:S(2)}) async-start(bf16[128,128,256]{2,1,0:T(8,128)(2,1)} %maximum_select_fusion), calls=%async_computation | async-start | bytes 16777216 | tf_op jit(solution)/shard_map/all_to_all | solution.py:51
  36.3 224.0 %all-gather.5.cloned.1.call-start = ((), (), s32[]{:S(2)}) async-start(), calls=%async_computation.3 | async-start | bytes 1179648 | tf_op jit(solution)/shard_map/all_gather | solution.py:79
  202.2 9.4 copy-start.2
  220.9 124.5 %reduce-scatter.3.cloned.1.call-start = ((), (), s32[]{:S(2)}) async-start(), calls=%async_computation.4 | async-start | bytes 4456448 | tf_op jit(solution)/shard_map/reduce_scatter | solution.py:80
  265.0 0.7 copy-start.6
  265.0 80.4 %copy-start.4 = (bf16[64,1024]{1,0:T(8,128)(2,1)S(1)}, bf16[64,1024]{1,0:T(8,128)(2,1)}, u32[]{:S(2)}) copy-start(bf16[64,1024]{1,0:T(8,128)(2,1)} %param.19) | copy-start | bytes 393220
  265.0 147.0 %all-gather.7.cloned.1.call-start = ((), (), s32[]{:S(2)}) async-start(), calls=%async_computation.5 | async-start | bytes 2228224 | tf_op jit(solution)/shard_map/all_gather | solution.py:91
  367.0 636.4 %all-reduce.2.cloned.1.call-start = ((), (), s32[]{:S(2)}) async-start(), calls=%async_computation.6 | async-start | bytes 29360128 | tf_op jit(solution)/shard_map/psum | solution.py:96
  412.0 6.8 copy-start.7
  412.0 6.8 copy-start.8
  428.5 669.0 %reduce-scatter.5.cloned.1.call-start = ((), (), s32[]{:S(2)}) async-start(), calls=%async_computation.7 | async-start | bytes 4456448 | tf_op jit(solution)/shard_map/reduce_scatter | solution.py:99
  1003.3 95.9 %copy-start.1 = (bf16[8,1024,128]{2,1,0:T(8,128)(2,1)S(1)}, bf16[8,1024,128]{2,1,0:T(8,128)(2,1)}, u32[]{:S(2)}) copy-start(bf16[8,1024,128]{2,1,0:T(8,128)(2,1)} %param.14) | copy-start | bytes 6291460
  1015.6 81.9 %copy-start.3 = (f32[64,1024]{1,0:T(8,128)S(1)}, f32[64,1024]{1,0:T(8,128)}, u32[]{:S(2)}) copy-start(f32[64,1024]{1,0:T(8,128)} %reduce-scatter.3.cloned.1.call-done) | copy-start | bytes 786436
Sparse Core Ops, SparseCore 0:
  221.0 39.2 all-gather.4
  265.1 80.1 reduce-scatter.2
  367.1 44.8 all-gather.6
  428.6 574.6 all-reduce.1
  1015.8 81.6 reduce-scatter.4
where the time goes:
time: 1110 us
  waiting for transfers between devices  820 us (74%)
  blocking collectives  166 us (15%)
  matrix products  46.4 us (4%)
  other arithmetic  28.8 us (3%)
  local copies, waits for them, and re-layouts  18.7 us (2%)
  between operations  13.3 us (1%)
  starting transfers between devices  12.1 us (1%)
    psum x1, waiting for transfers between devices, local(): summed = lax.psum(partials, 'col')  575 us
    all_gather x1, blocking collectives, local(): piece_values = lax.all_gather(own_values, 'col', axis=0, tiled=True)  118 us
    reduce_scatter x1, waiting for transfers between devices, local(): lax.psum_scatter(down_terms, 'row', scatter_dimension=0, tiled=True)  81.9 us
    reduce_scatter x1, waiting for transfers between devices, local(): lax.psum_scatter(jnp.dot(all_attended, out_weight, preferred_element_type...  79.7 us
    all_gather x1, waiting for transfers between devices, local(): block_piece = lax.all_gather(normed, 'row', axis=0, tiled=True)  44.7 us
    all_gather x1, waiting for transfers between devices, local(): all_attended = lax.all_gather(attended, 'col', axis=0, tiled=True)  39.3 us
    all_gather x1, blocking collectives, local(): piece_keys = lax.all_gather(own_keys, 'col', axis=0, tiled=True)  28.9 us
  transfers between devices with their start and end apart: 6, of which 5 were waited for; matrix products, arithmetic and copies ran while one was open for 0% of the time, Pallas kernels for 0%

commit v1 on v0

--- a/solution.py
+++ b/solution.py
@@ -62,8 +62,15 @@
     query_pos = col_index * BLK + jnp.arange(BLK * heads_here, dtype=jnp.int32) // heads_here
     own_keys = lax.dynamic_index_in_dim(stretch_keys, my_group, 0, keepdims=False)
     own_values = lax.dynamic_index_in_dim(stretch_values, my_group, 0, keepdims=False)
-    piece_keys = lax.all_gather(own_keys, "col", axis=0, tiled=True)
-    piece_values = lax.all_gather(own_values, "col", axis=0, tiled=True)
+
+    def _follow_vectors(field_in, point, mesh_ax):
+        return jnp.split(
+            lax.all_gather(jnp.concatenate([field_in, point], axis=1), mesh_ax, axis=0, tiled=True),
+            [field_in.shape[1]],
+            axis=1,
+        )
+
+    piece_keys, piece_values = _follow_vectors(own_keys, own_values, "col")
     scores = jnp.dot(query_rows, piece_keys.T, preferred_element_type=jnp.float32) * scaling
     key_pos = jnp.arange(piece_keys.shape[0], dtype=jnp.int32)
     allowed = key_pos[None, :] <= query_pos[:, None]

time: 1110 us -> 1080 us (0.973)
  blocking collectives: 166 us -> 139 us
    all_gather x2 -> x1, blocking collectives: 147 us -> 120 us  [_follow_vectors(): lax.all_gather(jnp.concatenate([field_in, point], axis=1), mesh_ax, axis=...]
where the time goes in v1:
time: 1080 us
  waiting for transfers between devices  821 us (76%)
  blocking collectives  139 us (13%)
  matrix products  46.4 us (4%)
  other arithmetic  28.8 us (3%)
  local copies, waits for them, and re-layouts  18.7 us (2%)
  between operations  13.3 us (1%)
  starting transfers between devices  12.1 us (1%)
    psum x1, waiting for transfers between devices, local(): summed = lax.psum(partials, 'col')  575 us
    all_gather x1, blocking collectives, _follow_vectors(): lax.all_gather(jnp.concatenate([field_in, point], axis=1), mesh_ax, axis=...  120 us
    reduce_scatter x1, waiting for transfers between devices, local(): lax.psum_scatter(down_terms, 'row', scatter_dimension=0, tiled=True)  81.9 us
    reduce_scatter x1, waiting for transfers between devices, local(): lax.psum_scatter(jnp.dot(all_attended, out_weight, preferred_element_type...  79.7 us
    all_gather x1, waiting for transfers between devices, local(): block_piece = lax.all_gather(normed, 'row', axis=0, tiled=True)  44.7 us
    all_gather x1, waiting for transfers between devices, local(): all_attended = lax.all_gather(attended, 'col', axis=0, tiled=True)  39.5 us
  transfers between devices with their start and end apart: 6, of which 5 were waited for; matrix products, arithmetic and copies ran while one was open for 0% of the time, Pallas kernels for 0%

profile of v1, /device:TPU:0, one launch (start us, length us, event | category | flops | bytes accessed | tf_op | source)
XLA Modules:
  0.0 1078.8 jit_solution(8922365992001146458)
XLA Ops:
  6.6 1.9 gather_fusion
  8.7 3.1 gather_fusion.2
  11.8 4.6 gather_fusion.1
  16.4 8.2 maximum_select_fusion
  24.6 11.7 %all-to-all-start = ((bf16[128,128,256]{2,1,0:T(8,128)(2,1)}), bf16[128,128,256]{2,1,0:T(8,128)(2,1)}, u32[]{:S(2)}, u32[]{:S(2)}) async-start(bf16[128,128,256]{2,1,0:T(8,128)(2,1)} %maximum_select_fusion), calls=%async_computation | async-start | bytes 16777216 | tf_op jit(solution)/shard_map/all_to_all | solution.py:51
  36.4 0.7 fusion.41
  37.2 0.8 dynamic-slice_bitcast_fusion
  38.0 120.0 %all_gather.9 = bf16[1024,256]{1,0:T(8,128)(2,1)S(1)} all-gather(bf16[128,256]{1,0:T(8,128)(2,1)S(1)} %pad_maximum_fusion.1), channel_id=1, replica_groups=mesh['row'=16,'col'=8] {'col'}, dimensions={0}, use_global_device_ids=true | all-gather | bytes 589824 | tf_op jit(solution)/shard_map/all_gather | solution.py:68
  158.0 0.8 copy-done.5
  158.8 0.5 fusion.10
  159.3 6.1 gather_fusion.3
  165.4 9.6 multiply_reduce_fusion
  175.1 8.8 fusion
  183.8 0.6 fusion.11
  184.5 7.8 fusion.15
  192.3 0.8 fusion.14
  193.0 0.7 reshape.273
  193.9 39.5 %all-gather.3.cloned.1.call-done = bf16[1024,512]{1,0:T(8,128)(2,1)} async-done(((bf16[128,512]{1,0:T(8,128)(2,1)}), bf16[1024,512]{1,0:T(8,128)(2,1)}) %all-gather.3.cloned.1.call-update) | async-done | bytes 1048592 | tf_op jit(solution)/shard_map/all_gather | solution.py:86
  233.3 4.7 fusion.50
  238.2 0.6 copy-done.8
  238.8 79.7 %reduce-scatter.3.cloned.1.call-done = f32[64,1024]{1,0:T(8,128)} async-done(((f32[1024,1024]{1,0:T(8,128)}), f32[64,1024]{1,0:T(8,128)}) %reduce-scatter.3.cloned.1.call-update) | async-done | bytes 262160 | tf_op jit(solution)/shard_map/reduce_scatter | solution.py:87
  318.5 1.1 multiply_reduce_fusion.1
  319.5 18.8 %psum.14 = f32[64]{0:T(128)S(1)} all-reduce(f32[64]{0:T(128)S(1)} %multiply_reduce_fusion.1), channel_id=1, replica_groups=mesh['row'=16,'col'=8] {'col'}, use_global_device_ids=true, to_apply=%region_8.9 | all-reduce | flops 64 | bytes 512 | tf_op jit(solution)/shard_map/psum | solution.py:94
  338.3 1.7 multiply_convert_fusion
  340.3 44.7 %all-gather.5.cloned.1.call-done = bf16[1024,1024]{1,0:T(8,128)(2,1)} async-done(((bf16[64,1024]{1,0:T(8,128)(2,1)}), bf16[1024,1024]{1,0:T(8,128)(2,1)}) %all-gather.5.cloned.1.call-update) | async-done | bytes 2097168 | tf_op jit(solution)/shard_map/all_gather | solution.py:98
  385.1 6.8 fusion.52
  391.9 4.0 fusion.51
  395.8 5.8 pad_maximum_fusion
  401.6 574.8 %all-reduce.2.cloned.1.call-done = f32[1024,3584]{1,0:T(8,128)} async-done(((f32[1024,3584]{1,0:T(8,128)}), f32[1024,3584]{1,0:T(8,128)}) %all-reduce.2.cloned.1.call-update) | async-done | bytes 14680080 | tf_op jit(solution)/shard_map/psum | solution.py:103
  976.4 12.3 %fusion.5 = f32[1024,1024]{1,0:T(8,128)} fusion(bf16[1792,1024]{1,0:T(8,128)(2,1)} %param.23, f32[1024,3584]{1,0:T(8,128)} %all-reduce.2.cloned.1.call-done), kind=kOutput, calls=%fused_computation.13 | convolution fusion | flops 3769106432 | bytes 22544384 | tf_op jit(solution)/shard_map/dot_general | solution.py:105
  988.8 81.9 %reduce-scatter.5.cloned.1.call-done = f32[64,1024]{1,0:T(8,128)} async-done(((f32[1024,1024]{1,0:T(8,128)}), f32[64,1024]{1,0:T(8,128)}) %reduce-scatter.5.cloned.1.call-update) | async-done | bytes 262160 | tf_op jit(solution)/shard_map/reduce_scatter | solution.py:106
  1070.6 1.6 add_convert_fusion
  (44 shorter events, 1.0 us)
Async XLA Ops:
  6.5 2.2 copy-start
  24.6 11.8 %copy-start.7 = (bf16[128,512]{1,0:T(8,128)(2,1)S(1)}, bf16[128,512]{1,0:T(8,128)(2,1)}, u32[]{:S(2)}) copy-start(bf16[128,512]{1,0:T(8,128)(2,1)} %param.12) | copy-start | bytes 393220
  24.6 134.7 %all-to-all-start = ((bf16[128,128,256]{2,1,0:T(8,128)(2,1)}), bf16[128,128,256]{2,1,0:T(8,128)(2,1)}, u32[]{:S(2)}, u32[]{:S(2)}) async-start(bf16[128,128,256]{2,1,0:T(8,128)(2,1)} %maximum_select_fusion), calls=%async_computation | async-start | bytes 16777216 | tf_op jit(solution)/shard_map/all_to_all | solution.py:51
  36.3 197.1 %all-gather.3.cloned.1.call-start = ((), (), s32[]{:S(2)}) async-start(), calls=%async_computation.3 | async-start | bytes 1179648 | tf_op jit(solution)/shard_map/all_gather | solution.py:86
  158.0 0.8 copy-start.5
  175.1 9.4 copy-start.2
  184.5 7.8 copy-start.6
  193.8 124.6 %reduce-scatter.3.cloned.1.call-start = ((), (), s32[]{:S(2)}) async-start(), calls=%async_computation.4 | async-start | bytes 4456448 | tf_op jit(solution)/shard_map/reduce_scatter | solution.py:87
  238.1 0.7 copy-start.8
  238.1 80.4 %copy-start.4 = (bf16[64,1024]{1,0:T(8,128)(2,1)S(1)}, bf16[64,1024]{1,0:T(8,128)(2,1)}, u32[]{:S(2)}) copy-start(bf16[64,1024]{1,0:T(8,128)(2,1)} %param.19) | copy-start | bytes 393220
  238.1 146.9 %all-gather.5.cloned.1.call-start = ((), (), s32[]{:S(2)}) async-start(), calls=%async_computation.5 | async-start | bytes 2228224 | tf_op jit(solution)/shard_map/all_gather | solution.py:98
  340.1 636.4 %all-reduce.2.cloned.1.call-start = ((), (), s32[]{:S(2)}) async-start(), calls=%async_computation.6 | async-start | bytes 29360128 | tf_op jit(solution)/shard_map/psum | solution.py:103
  385.0 6.8 copy-start.9
  385.1 6.8 copy-start.10
  401.6 669.0 %reduce-scatter.5.cloned.1.call-start = ((), (), s32[]{:S(2)}) async-start(), calls=%async_computation.7 | async-start | bytes 4456448 | tf_op jit(solution)/shard_map/reduce_scatter | solution.py:106
  976.4 95.9 %copy-start.1 = (bf16[8,1024,128]{2,1,0:T(8,128)(2,1)S(1)}, bf16[8,1024,128]{2,1,0:T(8,128)(2,1)}, u32[]{:S(2)}) copy-start(bf16[8,1024,128]{2,1,0:T(8,128)(2,1)} %param.14) | copy-start | bytes 6291460
  988.7 81.9 %copy-start.3 = (f32[64,1024]{1,0:T(8,128)S(1)}, f32[64,1024]{1,0:T(8,128)}, u32[]{:S(2)}) copy-start(f32[64,1024]{1,0:T(8,128)} %reduce-scatter.3.cloned.1.call-done) | copy-start | bytes 786436
Sparse Core Ops, SparseCore 0:
  193.9 39.3 all-gather.2
  238.2 80.1 reduce-scatter.2
  340.2 44.8 all-gather.4
  401.7 574.6 all-reduce.1
  988.9 81.6 reduce-scatter.4
